TPU v7x, 32 devices: a whole 2x2x4 slice. The times are simulated.
32 devices in a mesh: fsdp: 4 (over z), ctx: 2 (over x), tp: 4 (over y, core).
Axes of the slice: x: 2, y: 2, z: 4, core: 2. Of those that a mesh axis runs over, the one named last changes fastest.
Arguments:
- layer_in: bfloat16 [8, 1024, 1024], P('fsdp', ('ctx', 'tp')), may hold values from -6 to 6
- attn_gain: bfloat16 [1024], replicated, may hold values from 0.5 to 1.5
- ffn_gain: bfloat16 [1024], replicated, may hold values from 0.5 to 1.5
- query_weight: bfloat16 [1024, 1024], P(('fsdp', 'ctx'), 'tp'), may hold values from -0.1875 to 0.1875
- key_weight: bfloat16 [1024, 1024], P(('fsdp', 'ctx'), 'tp'), may hold values from -0.1875 to 0.1875
- value_weight: bfloat16 [1024, 1024], P(('fsdp', 'ctx'), 'tp'), may hold values from -0.1875 to 0.1875
- out_weight: bfloat16 [1024, 1024], P(('fsdp', 'ctx'), 'tp'), may hold values from -0.75 to 0.75
- variate_bias: float32 [2, 16], P(None, 'tp'), may hold values from -4 to 4
- gate_weight: bfloat16 [1024, 4096], P(('fsdp', 'ctx'), 'tp'), may hold values from -0.1875 to 0.1875
- up_weight: bfloat16 [1024, 4096], P(('fsdp', 'ctx'), 'tp'), may hold values from -0.1875 to 0.1875
- down_weight: bfloat16 [1024, 4096], P(('fsdp', 'ctx'), 'tp'), may hold values from -0.09375 to 0.09375
- segment_ids: int32 [8, 1024], P('fsdp'), may hold values from 0 to 15, never falling along the last dimension, each value on 1 to 512 neighbouring positions
- variate_ids: int32 [8, 1024], P('fsdp'), may hold values from 0 to 3
- time_ids: int32 [8, 1024], P('fsdp'), may hold values from 0 to 1023
- out_grad: bfloat16 [8, 1024, 1024], P('fsdp', ('ctx', 'tp')), may hold values from -6 to 6
Outputs:
- layer_out: bfloat16 [8, 1024, 1024], P('fsdp', ('ctx', 'tp'))
- in_grad: bfloat16 [8, 1024, 1024], P('fsdp', ('ctx', 'tp'))
- attn_gain_grad: float32 [1024], replicated
- ffn_gain_grad: float32 [1024], replicated
- query_grad: float32 [1024, 1024], P(('fsdp', 'ctx'), 'tp')
- key_grad: float32 [1024, 1024], P(('fsdp', 'ctx'), 'tp')
- value_grad: float32 [1024, 1024], P(('fsdp', 'ctx'), 'tp')
- out_weight_grad: float32 [1024, 1024], P(('fsdp', 'ctx'), 'tp')
- bias_grad: float32 [2, 16], P(None, 'tp')
- gate_grad: float32 [1024, 4096], P(('fsdp', 'ctx'), 'tp')
- up_grad: float32 [1024, 4096], P(('fsdp', 'ctx'), 'tp')
- down_grad: float32 [1024, 4096], P(('fsdp', 'ctx'), 'tp')
All inputs are finite; a program needn't handle non-finite values.
Results may differ from a plain program's by a relative error of at most 0.019.
Values may be sent and summed in bfloat16 or wider, within the bound.
No kernel may reach another device: no remote copies, remote signals or barrier semaphores. Data moves between devices by JAX's collectives and lax.ppermute only.
A program may use at most 128 MiB of HBM per device.

v0:
```python
import jax
import jax.numpy as jnp
from jax import lax
from jax.sharding import PartitionSpec as P

HEADS = 16
HEAD = 64
EPS = 1e-05
NEG = -1e30


def rms_norm(values, gain):
    return values * lax.rsqrt(jnp.mean(values * values, axis=-1, keepdims=True) + EPS) * gain


def rotate(values, time_rows):
    half_dim = values.shape[-1] // 2
    frequency = 10000.0 ** (-2.0 * jnp.arange(half_dim, dtype=jnp.float32) / values.shape[-1])
    angles = time_rows.astype(jnp.float32)[..., None, None] * frequency
    cosine = jnp.cos(angles)
    sine_part = jnp.sin(angles)
    first_half = values[..., :half_dim]
    second = values[..., half_dim:]
    return jnp.concatenate(
        [first_half * cosine - second * sine_part, second * cosine + first_half * sine_part],
        axis=-1,
    )


def swiglu(gate_vals, up_vals):
    return jax.nn.silu(gate_vals) * up_vals


def gather_rows(values):
    return lax.all_gather(values, "tp", axis=1, tiled=True)


def scatter_rows(values):
    return lax.psum_scatter(values, "tp", scatter_dimension=1, tiled=True)


def shards(
    layer_in,
    attn_gain,
    ffn_gain,
    query_weight,
    key_weight,
    value_weight,
    out_weight,
    variate_bias,
    gate_weight,
    up_weight,
    down_weight,
    segment_ids,
    variate_ids,
    time_ids,
    out_grad,
):
    seq_count, share, width = layer_in.shape
    span = share * lax.axis_size("tp")
    seq_length = segment_ids.shape[1]
    offset = lax.axis_index("ctx") * span
    local_heads = variate_bias.shape[1]
    proj_width = local_heads * HEAD
    row_count = seq_count * span
    block = 512
    block_starts = jnp.arange(span // block, dtype=jnp.int32) * block
    scale = HEAD ** (-0.5)
    my_times = lax.dynamic_slice_in_dim(time_ids, offset, span, 1)
    my_variates = lax.dynamic_slice_in_dim(variate_ids, offset, span, 1)
    my_segments = lax.dynamic_slice_in_dim(segment_ids, offset, span, 1)
    bias_same = variate_bias[0]
    bias_diff = variate_bias[1]
    gain_one = attn_gain.astype(jnp.float32)
    gain_two = ffn_gain.astype(jnp.float32)
    inputs = layer_in.astype(jnp.float32)
    rows_one = gather_rows(rms_norm(inputs, gain_one).astype(jnp.bfloat16)).reshape(
        row_count, width
    )
    query_full, key_full, value_full, out_full = (
        lax.all_gather(query_weight, ("fsdp", "ctx"), axis=0, tiled=True),
        lax.all_gather(key_weight, ("fsdp", "ctx"), axis=0, tiled=True),
        lax.all_gather(value_weight, ("fsdp", "ctx"), axis=0, tiled=True),
        lax.all_gather(out_weight, ("fsdp", "ctx"), axis=0, tiled=True),
    )
    queries_raw = jnp.dot(rows_one, query_full, preferred_element_type=jnp.float32).reshape(
        seq_count, span, local_heads, HEAD
    )
    keys_raw = jnp.dot(rows_one, key_full, preferred_element_type=jnp.float32).reshape(
        seq_count, span, local_heads, HEAD
    )
    queries = rotate(queries_raw, my_times).astype(jnp.bfloat16)
    keys_mine = rotate(keys_raw, my_times).astype(jnp.bfloat16).reshape(seq_count, span, proj_width)
    values_mine = (
        jnp.dot(rows_one, value_full, preferred_element_type=jnp.float32)
        .astype(jnp.bfloat16)
        .reshape(seq_count, span, proj_width)
    )
    keys_all, values_all = (
        lax.all_gather(keys_mine, "ctx", axis=1, tiled=True),
        lax.all_gather(values_mine, "ctx", axis=1, tiled=True),
    )

    def scores_of(query_block, key_rows, query_var, key_var, query_seg, key_seg):
        raw = (
            jnp.einsum("qhd,khd->hqk", query_block, key_rows, preferred_element_type=jnp.float32)
            * scale
        )
        same = (query_var[:, None] == key_var[None, :])[None]
        raw = raw + jnp.where(same, bias_same[:, None, None], bias_diff[:, None, None])
        return (jnp.where((query_seg[:, None] == key_seg[None, :])[None], raw, NEG), same)

    mixed_parts = []
    lse_parts = []
    for seq in range(seq_count):
        key_rows = keys_all[seq].reshape(seq_length, local_heads, HEAD)
        value_rows = values_all[seq].reshape(seq_length, local_heads, HEAD)

        def forward_block(first, seq=seq, key_rows=key_rows, value_rows=value_rows):
            query_block = queries[seq]
            query_var = my_variates[seq]
            query_seg = my_segments[seq]
            scores, same = scores_of(
                query_block, key_rows, query_var, variate_ids[seq], query_seg, segment_ids[seq]
            )
            top = jnp.max(scores, axis=-1, keepdims=True)
            expo = jnp.exp(scores - top)
            total = jnp.sum(expo, axis=-1, keepdims=True)
            probs = (expo / total).astype(jnp.bfloat16)
            mixed_block = jnp.einsum(
                "hqk,khd->qhd", probs, value_rows, preferred_element_type=jnp.float32
            )
            return (
                mixed_block.astype(jnp.bfloat16).reshape(block, proj_width),
                top[..., 0] + jnp.log(total[..., 0]),
            )

        mixed_seq, lse_seq = lax.map(forward_block, block_starts)
        mixed_parts.append(mixed_seq.reshape(span, proj_width))
        lse_parts.append(lse_seq)
    mixed = jnp.stack(mixed_parts).reshape(row_count, proj_width)
    attn_part = jnp.einsum("rp,dp->rd", mixed, out_full, preferred_element_type=jnp.float32)
    hidden = inputs + scatter_rows(attn_part.reshape(seq_count, span, width))
    rows_two = gather_rows(rms_norm(hidden, gain_two).astype(jnp.bfloat16)).reshape(
        row_count, width
    )
    gate_full, up_full, down_full = (
        lax.all_gather(gate_weight, ("fsdp", "ctx"), axis=0, tiled=True),
        lax.all_gather(up_weight, ("fsdp", "ctx"), axis=0, tiled=True),
        lax.all_gather(down_weight, ("fsdp", "ctx"), axis=0, tiled=True),
    )
    gate = jnp.dot(rows_two, gate_full, preferred_element_type=jnp.float32)
    up_vals = jnp.dot(rows_two, up_full, preferred_element_type=jnp.float32)
    act = swiglu(gate, up_vals).astype(jnp.bfloat16)
    ffn_part = jnp.einsum("rf,df->rd", act, down_full, preferred_element_type=jnp.float32)
    layer_out = (hidden + scatter_rows(ffn_part.reshape(seq_count, span, width))).astype(
        jnp.bfloat16
    )
    query_back, key_back, value_back, out_back = (
        lax.all_gather(query_weight, ("fsdp", "ctx"), axis=0, tiled=True),
        lax.all_gather(key_weight, ("fsdp", "ctx"), axis=0, tiled=True),
        lax.all_gather(value_weight, ("fsdp", "ctx"), axis=0, tiled=True),
        lax.all_gather(out_weight, ("fsdp", "ctx"), axis=0, tiled=True),
    )
    gate_back, up_back, down_back = (
        lax.all_gather(gate_weight, ("fsdp", "ctx"), axis=0, tiled=True),
        lax.all_gather(up_weight, ("fsdp", "ctx"), axis=0, tiled=True),
        lax.all_gather(down_weight, ("fsdp", "ctx"), axis=0, tiled=True),
    )
    grad_rows = gather_rows(out_grad).reshape(row_count, width)
    d_act = jnp.dot(grad_rows, down_back, preferred_element_type=jnp.float32)
    down_local = jnp.einsum("rd,rf->df", grad_rows, act, preferred_element_type=jnp.float32)
    swiglu_pull = jax.vjp(swiglu, gate, up_vals)[1]
    d_gate, d_up = swiglu_pull(d_act)
    d_gate = d_gate.astype(jnp.bfloat16)
    d_up = d_up.astype(jnp.bfloat16)
    gate_local = jnp.einsum("rd,rf->df", rows_two, d_gate, preferred_element_type=jnp.float32)
    up_local = jnp.einsum("rd,rf->df", rows_two, d_up, preferred_element_type=jnp.float32)
    d_normed_two = jnp.einsum("rf,df->rd", d_gate, gate_back, preferred_element_type=jnp.float32)
    d_normed_two = d_normed_two + jnp.einsum(
        "rf,df->rd", d_up, up_back, preferred_element_type=jnp.float32
    )
    norm_two_pull = jax.vjp(rms_norm, hidden, gain_two)[1]
    d_hidden_norm, d_gain_two = norm_two_pull(
        scatter_rows(d_normed_two.reshape(seq_count, span, width))
    )
    d_hidden = out_grad.astype(jnp.float32) + d_hidden_norm
    branch_rows = gather_rows(d_hidden.astype(jnp.bfloat16)).reshape(row_count, width)
    out_local = jnp.einsum("rd,rp->dp", branch_rows, mixed, preferred_element_type=jnp.float32)
    d_mixed = jnp.dot(branch_rows, out_back, preferred_element_type=jnp.float32).astype(
        jnp.bfloat16
    )
    d_mixed = d_mixed.reshape(seq_count, span, local_heads, HEAD)
    d_query_parts = []
    d_key_parts = []
    d_value_parts = []
    d_bias = jnp.zeros((2, local_heads), jnp.float32)
    for seq in range(seq_count):
        key_rows = keys_all[seq].reshape(seq_length, local_heads, HEAD)
        value_rows = values_all[seq].reshape(seq_length, local_heads, HEAD)

        def back_block(carry, item, seq=seq, key_rows=key_rows, value_rows=value_rows):
            d_keys, d_values, bias_sum = carry
            first, lse_block = item
            query_block = queries[seq]
            query_var = my_variates[seq]
            query_seg = my_segments[seq]
            scores, same = scores_of(
                query_block, key_rows, query_var, variate_ids[seq], query_seg, segment_ids[seq]
            )
            probs = jnp.exp(scores - lse_block[:, :, None])
            probs_low = probs.astype(jnp.bfloat16)
            d_out = d_mixed[seq]
            d_probs = jnp.einsum(
                "qhd,khd->hqk", d_out, value_rows, preferred_element_type=jnp.float32
            )
            delta = jnp.sum(probs * d_probs, axis=-1, keepdims=True)
            d_scores = (probs * (d_probs - delta)).astype(jnp.bfloat16)
            d_query = (
                jnp.einsum("hqk,khd->qhd", d_scores, key_rows, preferred_element_type=jnp.float32)
                * scale
            )
            d_keys = (
                d_keys
                + jnp.einsum(
                    "hqk,qhd->khd", d_scores, query_block, preferred_element_type=jnp.float32
                )
                * scale
            )
            d_values = d_values + jnp.einsum(
                "hqk,qhd->khd", probs_low, d_out, preferred_element_type=jnp.float32
            )
            wide_scores = d_scores.astype(jnp.float32)
            same_sum = jnp.sum(jnp.where(same, wide_scores, 0.0), axis=(1, 2))
            diff_sum = jnp.sum(jnp.where(same, 0.0, wide_scores), axis=(1, 2))
            return ((d_keys, d_values, bias_sum + jnp.stack([same_sum, diff_sum])), d_query)

        zero_rows = jnp.zeros((seq_length, local_heads, HEAD), jnp.float32)
        (d_keys, d_values, bias_sum), d_query_blocks = lax.scan(
            back_block,
            (zero_rows, zero_rows, jnp.zeros((2, local_heads), jnp.float32)),
            (block_starts, lse_parts[seq]),
        )
        d_query_parts.append(d_query_blocks.reshape(span, local_heads, HEAD))
        d_key_parts.append(d_keys.reshape(seq_length, proj_width))
        d_value_parts.append(d_values.reshape(seq_length, proj_width))
        d_bias = d_bias + bias_sum
    d_keys_mine, d_values_mine = (
        lax.psum_scatter(
            jnp.stack(d_key_parts).astype(jnp.bfloat16), "ctx", scatter_dimension=1, tiled=True
        ).astype(jnp.float32),
        lax.psum_scatter(
            jnp.stack(d_value_parts).astype(jnp.bfloat16), "ctx", scatter_dimension=1, tiled=True
        ).astype(jnp.float32),
    )

    def rope_local(values):
        return rotate(values, my_times)

    rope_pull = jax.vjp(rope_local, queries_raw)[1]
    d_query_raw = (
        rope_pull(jnp.stack(d_query_parts))[0].astype(jnp.bfloat16).reshape(row_count, proj_width)
    )
    d_key_raw = (
        rope_pull(d_keys_mine.reshape(seq_count, span, local_heads, HEAD))[0]
        .astype(jnp.bfloat16)
        .reshape(row_count, proj_width)
    )
    d_value_low = d_values_mine.astype(jnp.bfloat16).reshape(row_count, proj_width)
    query_local = jnp.einsum("rd,rp->dp", rows_one, d_query_raw, preferred_element_type=jnp.float32)
    key_local = jnp.einsum("rd,rp->dp", rows_one, d_key_raw, preferred_element_type=jnp.float32)
    value_local = jnp.einsum("rd,rp->dp", rows_one, d_value_low, preferred_element_type=jnp.float32)
    d_normed_one = jnp.einsum(
        "rp,dp->rd", d_query_raw, query_back, preferred_element_type=jnp.float32
    )
    d_normed_one = d_normed_one + jnp.einsum(
        "rp,dp->rd", d_key_raw, key_back, preferred_element_type=jnp.float32
    )
    d_normed_one = d_normed_one + jnp.einsum(
        "rp,dp->rd", d_value_low, value_back, preferred_element_type=jnp.float32
    )
    norm_one_pull = jax.vjp(rms_norm, inputs, gain_one)[1]
    d_input_norm, d_gain_one = norm_one_pull(
        scatter_rows(d_normed_one.reshape(seq_count, span, width))
    )
    in_grad = (d_hidden + d_input_norm).astype(jnp.bfloat16)
    query_grad, key_grad, value_grad, out_weight_grad = (
        lax.psum_scatter(
            query_local.astype(jnp.bfloat16), ("fsdp", "ctx"), scatter_dimension=0, tiled=True
        ).astype(jnp.float32),
        lax.psum_scatter(
            key_local.astype(jnp.bfloat16), ("fsdp", "ctx"), scatter_dimension=0, tiled=True
        ).astype(jnp.float32),
        lax.psum_scatter(
            value_local.astype(jnp.bfloat16), ("fsdp", "ctx"), scatter_dimension=0, tiled=True
        ).astype(jnp.float32),
        lax.psum_scatter(
            out_local.astype(jnp.bfloat16), ("fsdp", "ctx"), scatter_dimension=0, tiled=True
        ).astype(jnp.float32),
    )
    gate_grad, up_grad, down_grad = (
        lax.psum_scatter(
            gate_local.astype(jnp.bfloat16), ("fsdp", "ctx"), scatter_dimension=0, tiled=True
        ).astype(jnp.float32),
        lax.psum_scatter(
            up_local.astype(jnp.bfloat16), ("fsdp", "ctx"), scatter_dimension=0, tiled=True
        ).astype(jnp.float32),
        lax.psum_scatter(
            down_local.astype(jnp.bfloat16), ("fsdp", "ctx"), scatter_dimension=0, tiled=True
        ).astype(jnp.float32),
    )
    head_offset = lax.axis_index("tp") * local_heads
    bias_full = lax.dynamic_update_slice_in_dim(
        jnp.zeros((2, HEADS), jnp.float32), d_bias, head_offset, 1
    )
    attn_gain_grad, ffn_gain_grad, bias_total = lax.psum(
        (d_gain_one, d_gain_two, bias_full), ("fsdp", "ctx", "tp")
    )
    bias_grad = lax.dynamic_slice_in_dim(bias_total, head_offset, local_heads, 1)
    return (
        layer_out,
        in_grad,
        attn_gain_grad,
        ffn_gain_grad,
        query_grad,
        key_grad,
        value_grad,
        out_weight_grad,
        bias_grad,
        gate_grad,
        up_grad,
        down_grad,
    )


def solution(mesh):
    in_specs = (
        P("fsdp", ("ctx", "tp"), None),
        P(),
        P(),
        P(("fsdp", "ctx"), "tp"),
        P(("fsdp", "ctx"), "tp"),
        P(("fsdp", "ctx"), "tp"),
        P(("fsdp", "ctx"), "tp"),
        P(None, "tp"),
        P(("fsdp", "ctx"), "tp"),
        P(("fsdp", "ctx"), "tp"),
        P(("fsdp", "ctx"), "tp"),
        P("fsdp", None),
        P("fsdp", None),
        P("fsdp", None),
        P("fsdp", ("ctx", "tp"), None),
    )
    out_specs = (
        P("fsdp", ("ctx", "tp"), None),
        P("fsdp", ("ctx", "tp"), None),
        P(),
        P(),
        P(("fsdp", "ctx"), "tp"),
        P(("fsdp", "ctx"), "tp"),
        P(("fsdp", "ctx"), "tp"),
        P(("fsdp", "ctx"), "tp"),
        P(None, "tp"),
        P(("fsdp", "ctx"), "tp"),
        P(("fsdp", "ctx"), "tp"),
        P(("fsdp", "ctx"), "tp"),
    )
    return jax.shard_map(shards, mesh=mesh, in_specs=in_specs, out_specs=out_specs, check_vma=False)
```

profile of v0, /device:TPU:0, one launch (start us, length us, event | category | flops | bytes accessed | tf_op | source)
XLA Modules:
  0.0 1151.3 jit_solution(9747962312075755871)
XLA Ops:
  15.6 33.3 %all_gather.49 = bf16[1024,256]{1,0:T(8,128)(2,1)S(1)} all-gather(bf16[128,256]{1,0:T(8,128)(2,1)} %param.18), channel_id=1, replica_groups=mesh['fsdp'=4,'ctx'=2,'tp'=4] {'fsdp','ctx'}, dimensions={0}, use_global_device_ids=true | all-gather | bytes 589824 | tf_op jit(solution)/shard_map/all_gather | solution.py:81
  48.9 31.6 %all_gather.50 = bf16[1024,256]{1,0:T(8,128)(2,1)S(1)} all-gather(bf16[128,256]{1,0:T(8,128)(2,1)} %param.19), channel_id=1, replica_groups=mesh['fsdp'=4,'ctx'=2,'tp'=4] {'fsdp','ctx'}, dimensions={0}, use_global_device_ids=true | all-gather | bytes 589824 | tf_op jit(solution)/shard_map/all_gather | solution.py:82
  80.5 31.9 %all_gather.47 = bf16[1024,256]{1,0:T(8,128)(2,1)S(1)} all-gather(bf16[128,256]{1,0:T(8,128)(2,1)} %param.20), channel_id=1, replica_groups=mesh['fsdp'=4,'ctx'=2,'tp'=4] {'fsdp','ctx'}, dimensions={0}, use_global_device_ids=true | all-gather | bytes 589824 | tf_op jit(solution)/shard_map/all_gather | solution.py:83
  112.3 31.6 %all_gather.52 = bf16[1024,256]{1,0:T(8,128)(2,1)S(1)} all-gather(bf16[128,256]{1,0:T(8,128)(2,1)} %param.21), channel_id=1, replica_groups=mesh['fsdp'=4,'ctx'=2,'tp'=4] {'fsdp','ctx'}, dimensions={0}, use_global_device_ids=true | all-gather | bytes 589824 | tf_op jit(solution)/shard_map/all_gather | solution.py:84
  144.9 3.3 convolution_convert_fusion.5
  148.7 2.5 fusion.20
  156.3 14.2 %all-gather.12.cloned.1.call-done = bf16[2,1024,256]{2,1,0:T(8,128)(2,1)} async-done(((bf16[2,512,256]{2,1,0:T(8,128)(2,1)}), bf16[2,1024,256]{2,1,0:T(8,128)(2,1)}) %all-gather.12.cloned.1.call-update) | async-done | bytes 1048592 | tf_op jit(solution)/shard_map/all_gather | solution.py:101
  170.6 2.2 fusion.65
  172.8 2.0 copy.51
  174.8 2.0 copy.54
  176.9 17.1 %all-gather.14.cloned.1.call-done = bf16[2,1024,256]{1,2,0:T(8,128)(2,1)} async-done(((bf16[2,512,256]{1,2,0:T(8,128)(2,1)}), bf16[2,1024,256]{1,2,0:T(8,128)(2,1)}) %all-gather.14.cloned.1.call-update) | async-done | bytes 1048592 | tf_op jit(solution)/shard_map/all_gather | solution.py:100
  194.0 2.1 fusion.64
  196.1 4.1 fusion.69
  203.5 2.8 fusion.38
  207.4 4.2 fusion.70
  214.9 2.1 fusion.39
  217.3 2.7 fusion.48
  221.1 43.6 %reduce-scatter.16.cloned.1.call-done = f32[2,128,1024]{2,1,0:T(8,128)} async-done(((f32[2,512,1024]{2,1,0:T(8,128)}), f32[2,128,1024]{2,1,0:T(8,128)}) %reduce-scatter.16.cloned.1.call-update) | async-done | bytes 1048592 | tf_op jit(solution)/shard_map/reduce_scatter | solution.py:39
  269.3 2.9 all-gather.20.cloned.1.call-done
  272.2 23.0 %all-gather.16.cloned.1.call-done = bf16[2,512,1024]{2,1,0:T(8,128)(2,1)} async-done(((bf16[2,128,1024]{2,1,0:T(8,128)(2,1)}), bf16[2,512,1024]{2,1,0:T(8,128)(2,1)}) %all-gather.16.cloned.1.call-update) | async-done | bytes 2097168 | tf_op jit(solution)/shard_map/all_gather | solution.py:35
  295.3 6.6 fusion.72
  301.8 45.0 %all-gather.18.cloned.1.call-done = bf16[1024,1024]{1,0:T(8,128)(2,1)} async-done(((bf16[128,1024]{1,0:T(8,128)(2,1)}), bf16[1024,1024]{1,0:T(8,128)(2,1)}) %all-gather.18.cloned.1.call-update) | async-done | bytes 2097168 | tf_op jit(solution)/shard_map/all_gather | solution.py:148
  346.9 6.5 fusion.71
  353.4 16.1 %all-gather.24.cloned.1.call-done = bf16[2,512,1024]{2,1,0:T(8,128)(2,1)} async-done(((bf16[2,128,1024]{2,1,0:T(8,128)(2,1)}), bf16[2,512,1024]{2,1,0:T(8,128)(2,1)}) %all-gather.24.cloned.1.call-update) | async-done | bytes 2097168 | tf_op jit(solution)/shard_map/all_gather | solution.py:35
  369.5 51.7 %all-gather.22.cloned.1.call-done = bf16[1024,1024]{1,0:T(8,128)(2,1)} async-done(((bf16[128,1024]{1,0:T(8,128)(2,1)}), bf16[1024,1024]{1,0:T(8,128)(2,1)}) %all-gather.22.cloned.1.call-update) | async-done | bytes 2097168 | tf_op jit(solution)/shard_map/all_gather | solution.py:150
  421.2 9.9 multiply_convert_fusion.2
  431.1 2.4 fusion.74
  434.2 4.4 convolution_add_fusion
  438.7 43.1 %reduce-scatter.20.cloned.1.call-done = f32[2,128,1024]{2,1,0:T(8,128)} async-done(((f32[2,512,1024]{2,1,0:T(8,128)}), f32[2,128,1024]{2,1,0:T(8,128)}) %reduce-scatter.20.cloned.1.call-update) | async-done | bytes 1048592 | tf_op jit(solution)/shard_map/reduce_scatter | solution.py:39
  481.8 2.1 multiply_reduce_fusion.2
  483.9 2.3 fusion.53
  486.5 22.2 %all-gather.26.cloned.1.call-done = bf16[2,512,1024]{2,1,0:T(8,128)(2,1)} async-done(((bf16[2,128,1024]{2,1,0:T(8,128)(2,1)}), bf16[2,512,1024]{2,1,0:T(8,128)(2,1)}) %all-gather.26.cloned.1.call-update) | async-done | bytes 2097168 | tf_op jit(solution)/shard_map/all_gather | solution.py:35
  508.7 2.4 convolution_convert_fusion.4
  511.2 5.8 fusion.24
  517.1 7.2 multiply_reduce_fusion.1
  524.3 2.3 fusion.27
  526.6 2.0 copy.60
  530.7 2.3 pad_maximum_fusion.1
  533.1 8.7 fusion
  543.3 2.6 multiply_reduce_fusion
  545.9 4.8 fusion.2
  554.9 6.0 convert_bitcast_fusion
  560.8 4.1 copy.67
  565.0 5.9 convolution_convert_fusion
  571.0 5.9 convolution_convert_fusion.1
  577.0 3.1 fusion.33
  580.2 4.5 fusion.36
  584.8 3.2 fusion.32
  588.3 4.5 fusion.37
  594.1 2.8 multiply_add_fusion.1
  602.8 3.2 convolution_convert_fusion.3
  608.7 2.7 add_add_fusion
  611.5 6.7 fusion.73
  618.3 29.3 %reduce-scatter.40.cloned.1.call-done = bf16[128,1024]{1,0:T(8,128)(2,1)} async-done(((bf16[1024,1024]{1,0:T(8,128)(2,1)}), bf16[128,1024]{1,0:T(8,128)(2,1)}) %reduce-scatter.40.cloned.1.call-update) | async-done | bytes 262160
  649.6 68.4 %reduce-scatter.38.cloned.1.call-done = bf16[128,1024]{1,0:T(8,128)(2,1)} async-done(((bf16[1024,1024]{1,0:T(8,128)(2,1)}), bf16[128,1024]{1,0:T(8,128)(2,1)}) %reduce-scatter.38.cloned.1.call-update) | async-done | bytes 262160 | tf_op jit(solution)/shard_map/reduce_scatter | solution.py:305
  719.8 68.3 %reduce-scatter.36.cloned.1.call-done = bf16[128,1024]{1,0:T(8,128)(2,1)} async-done(((bf16[1024,1024]{1,0:T(8,128)(2,1)}), bf16[128,1024]{1,0:T(8,128)(2,1)}) %reduce-scatter.36.cloned.1.call-update) | async-done | bytes 262160 | tf_op jit(solution)/shard_map/reduce_scatter | solution.py:302
  790.1 62.4 %reduce-scatter.34.cloned.1.call-done = bf16[128,256]{1,0:T(8,128)(2,1)} async-done(((bf16[1024,256]{1,0:T(8,128)(2,1)}), bf16[128,256]{1,0:T(8,128)(2,1)}) %reduce-scatter.34.cloned.1.call-update) | async-done | bytes 65552 | tf_op jit(solution)/shard_map/reduce_scatter | solution.py:297
  854.0 63.0 %reduce-scatter.32.cloned.1.call-done = bf16[128,256]{1,0:T(8,128)(2,1)} async-done(((bf16[1024,256]{1,0:T(8,128)(2,1)}), bf16[128,256]{1,0:T(8,128)(2,1)}) %reduce-scatter.32.cloned.1.call-update) | async-done | bytes 65552 | tf_op jit(solution)/shard_map/reduce_scatter | solution.py:294
  918.5 63.3 %reduce-scatter.30.cloned.1.call-done = bf16[128,256]{1,0:T(8,128)(2,1)} async-done(((bf16[1024,256]{1,0:T(8,128)(2,1)}), bf16[128,256]{1,0:T(8,128)(2,1)}) %reduce-scatter.30.cloned.1.call-update) | async-done | bytes 65552 | tf_op jit(solution)/shard_map/reduce_scatter | solution.py:291
  983.4 63.6 %reduce-scatter.28.cloned.1.call-done = bf16[128,256]{1,0:T(8,128)(2,1)} async-done(((bf16[1024,256]{1,0:T(8,128)(2,1)}), bf16[128,256]{1,0:T(8,128)(2,1)}) %reduce-scatter.28.cloned.1.call-update) | async-done | bytes 65552 | tf_op jit(solution)/shard_map/reduce_scatter | solution.py:288
  1048.4 44.4 %reduce-scatter.26.cloned.1.call-done = f32[2,128,1024]{2,1,0:T(8,128)} async-done(((f32[2,512,1024]{2,1,0:T(8,128)}), f32[2,128,1024]{2,1,0:T(8,128)}) %reduce-scatter.26.cloned.1.call-update) | async-done | bytes 1048592 | tf_op jit(solution)/shard_map/reduce_scatter | solution.py:39
  1094.4 39.8 %all-reduce.4 = (f32[1024]{0:T(1024)}, f32[1024]{0:T(1024)}, f32[2,16]{1,0:T(2,128)S(1)}) all-reduce(f32[1024]{0:T(1024)S(1)} %get-tuple-element.206, f32[1024]{0:T(1024)S(1)} %copy-done.44, f32[2,16]{1,0:T(2,128)S(1)} %dynamic_update_slice.18), channel_id=1, replica_groups=mesh['fsdp'=4,'ctx'=2,'tp'=4] {'fsdp','ctx','tp'}, use_global_device_ids=true, to_apply=%region_17.18 | all-reduce | flops 2080 | bytes 16640 | tf_op jit(solution)/shard_map/psum | solution.py:316
  1134.9 5.8 reduce-scatter.18.cloned.1.call-done
  1140.7 3.0 fusion.44
  (243 shorter events, 60.6 us)
Async XLA Ops:
  8.0 136.9 %all-gather.10.cloned.1.call-start = ((), (), s32[]{:S(2)}) async-start(), calls=%async_computation.13 | async-start | bytes 2621440 | tf_op jit(solution)/shard_map/all_gather | solution.py:35
  13.2 157.4 %all-gather.12.cloned.1.call-start = ((), (), s32[]{:S(2)}) async-start(), calls=%async_computation.14 | async-start | bytes 1572864 | tf_op jit(solution)/shard_map/all_gather | solution.py:101
  80.5 67.8 %copy-start.43 = (s32[2,1024]{1,0:T(2,128)S(1)}, s32[2,1024]{1,0:T(2,128)}, u32[]{:S(2)}) copy-start(s32[2,1024]{1,0:T(2,128)} %param.26) | copy-start | bytes 24580
  112.3 36.2 %copy-start.23 = (bf16[1024,256]{1,0:T(8,128)(2,1)}, bf16[1024,256]{1,0:T(8,128)(2,1)S(1)}, u32[]{:S(2)}) copy-start(bf16[1024,256]{1,0:T(8,128)(2,1)S(1)} %all_gather.47) | copy-start | bytes 1572868
  144.0 73.3 %copy-start.13 = (bf16[1024,256]{1,0:T(8,128)(2,1)}, bf16[1024,256]{1,0:T(8,128)(2,1)S(1)}, u32[]{:S(2)}) copy-start(bf16[1024,256]{1,0:T(8,128)(2,1)S(1)} %all_gather.52) | copy-start | bytes 1572868
  144.5 7.5 copy-start.25
  144.9 51.2 %copy-start.11 = (pred[512,1024]{1,0:T(8,128)(4,1)}, pred[512,1024]{1,0:T(8,128)(4,1)S(1)}, u32[]{:S(2)}) copy-start(pred[512,1024]{1,0:T(8,128)(4,1)S(1)} %broadcast_compare_fusion) | copy-start | bytes 1572868
  148.2 45.8 %all-gather.14.cloned.1.call-start = ((), (), s32[]{:S(2)}) async-start(), calls=%async_computation.15 | async-start | bytes 1572864 | tf_op jit(solution)/shard_map/all_gather | solution.py:100
  152.4 55.0 %copy-start.7 = (bf16[2,512,4,32]{1,3,2,0:T(8,128)(2,1)}, bf16[2,512,4,32]{1,3,2,0:T(8,128)(2,1)S(1)}, u32[]{:S(2)}) copy-start(bf16[2,512,4,32]{1,3,2,0:T(8,128)(2,1)S(1)} %get-tuple-element.238) | copy-start | bytes 786436
  152.4 55.0 %copy-start.9 = (bf16[2,512,4,32]{1,3,2,0:T(8,128)(2,1)}, bf16[2,512,4,32]{1,3,2,0:T(8,128)(2,1)S(1)}, u32[]{:S(2)}) copy-start(bf16[2,512,4,32]{1,3,2,0:T(8,128)(2,1)S(1)} %get-tuple-element.239) | copy-start | bytes 786436
  153.4 111.4 %reduce-scatter.16.cloned.1.call-start = ((), (), s32[]{:S(2)}) async-start(), calls=%async_computation.16 | async-start | bytes 5242880 | tf_op jit(solution)/shard_map/reduce_scatter | solution.py:39
  153.6 46.5 %copy-start.55 = (f32[4]{0:T(128)}, f32[4]{0:T(128)S(1)}, u32[]{:S(2)}) copy-start(f32[4]{0:T(128)S(1)} %get-tuple-element.264) | copy-start | bytes 52
  153.6 46.5 %copy-start.56 = (f32[4]{0:T(128)}, f32[4]{0:T(128)S(1)}, u32[]{:S(2)}) copy-start(f32[4]{0:T(128)S(1)} %get-tuple-element.265) | copy-start | bytes 52
  154.0 53.4 %copy-start.14 = (pred[512,1024]{1,0:T(8,128)(4,1)}, pred[512,1024]{1,0:T(8,128)(4,1)S(1)}, u32[]{:S(2)}) copy-start(pred[512,1024]{1,0:T(8,128)(4,1)S(1)} %broadcast_compare_fusion.2) | copy-start | bytes 1572868
  196.1 4.1 copy-start.22
  202.1 4.2 copy-start.35
  207.4 9.9 copy-start.27
  217.3 47.5 %copy-start.4 = (bf16[2,128,1024]{2,1,0:T(8,128)(2,1)S(1)}, bf16[2,128,1024]{2,1,0:T(8,128)(2,1)}, u32[]{:S(2)}) copy-start(bf16[2,128,1024]{2,1,0:T(8,128)(2,1)} %param.15) | copy-start | bytes 1572868
  220.0 52.2 %all-gather.20.cloned.1.call-start = ((), (), s32[]{:S(2)}) async-start(), calls=%async_computation.19 | async-start | bytes 2359296 | tf_op jit(solution)/shard_map/all_gather | solution.py:149
  220.6 74.7 %all-gather.16.cloned.1.call-start = ((), (), s32[]{:S(2)}) async-start(), calls=%async_computation.17 | async-start | bytes 2621440 | tf_op jit(solution)/shard_map/all_gather | solution.py:35
  221.1 262.7 %copy-start.31 = (f32[1024]{0:T(1024)}, f32[1024]{0:T(1024)S(1)}, u32[]{:S(2)}) copy-start(f32[1024]{0:T(1024)S(1)} %convert_element_type.167) | copy-start | bytes 12292
  266.2 217.6 %copy-start.41 = (f32[2,128]{1,0:T(2,128)}, f32[2,128]{1,0:T(2,128)S(1)}, u32[]{:S(2)}) copy-start(f32[2,128]{1,0:T(2,128)S(1)} %fusion.57) | copy-start | bytes 3076
  267.2 79.7 %all-gather.18.cloned.1.call-start = ((), (), s32[]{:S(2)}) async-start(), calls=%async_computation.18 | async-start | bytes 2359296 | tf_op jit(solution)/shard_map/all_gather | solution.py:148
  267.8 101.7 %all-gather.24.cloned.1.call-start = ((), (), s32[]{:S(2)}) async-start(), calls=%async_computation.22 | async-start | bytes 2621440 | tf_op jit(solution)/shard_map/all_gather | solution.py:35
  268.5 152.7 %all-gather.22.cloned.1.call-start = ((), (), s32[]{:S(2)}) async-start(), calls=%async_computation.20 | async-start | bytes 2359296 | tf_op jit(solution)/shard_map/all_gather | solution.py:150
  269.3 212.5 %reduce-scatter.20.cloned.1.call-start = ((), (), s32[]{:S(2)}) async-start(), calls=%async_computation.23 | async-start | bytes 5242880 | tf_op jit(solution)/shard_map/reduce_scatter | solution.py:39
  421.2 9.9 copy-start.60
  438.6 45.3 %copy-start.6 = (bf16[2,128,1024]{2,1,0:T(8,128)(2,1)S(1)}, bf16[2,128,1024]{2,1,0:T(8,128)(2,1)}, u32[]{:S(2)}) copy-start(bf16[2,128,1024]{2,1,0:T(8,128)(2,1)} %param.29) | copy-start | bytes 1572868
  438.6 47.9 %copy-start.36 = (f32[4,512]{1,0:T(4,128)S(1)}, f32[4,512]{1,0:T(4,128)}, u32[]{:S(2)}) copy-start(f32[4,512]{1,0:T(4,128)} %copy-done.35) | copy-start | bytes 24580
  438.6 47.9 %copy-start.38 = (f32[4,512]{1,0:T(4,128)S(1)}, f32[4,512]{1,0:T(4,128)}, u32[]{:S(2)}) copy-start(f32[4,512]{1,0:T(4,128)} %copy-done.37) | copy-start | bytes 24580
  438.6 47.9 %copy-start.40 = (f32[4,512]{1,0:T(4,128)S(1)}, f32[4,512]{1,0:T(4,128)}, u32[]{:S(2)}) copy-start(f32[4,512]{1,0:T(4,128)} %copy-done.39) | copy-start | bytes 24580
  438.6 70.1 %all-gather.26.cloned.1.call-start = ((), (), s32[]{:S(2)}) async-start(), calls=%async_computation.24 | async-start | bytes 2621440 | tf_op jit(solution)/shard_map/all_gather | solution.py:35
  483.8 24.9 %copy-start.49 = (f32[2,128]{1,0:T(2,128)}, f32[2,128]{1,0:T(2,128)S(1)}, u32[]{:S(2)}) copy-start(f32[2,128]{1,0:T(2,128)S(1)} %multiply_multiply_fusion.1) | copy-start | bytes 3076
  486.2 98.6 %reduce-scatter.24.cloned.1.call-start = ((), (), s32[]{:S(2)}) async-start(), calls=%async_computation.26 | async-start | bytes 1572864 | tf_op jit(solution)/shard_map/reduce_scatter | solution.py:252
  511.2 5.9 copy-start.18
  511.2 13.1 %slice-start = ((s8[8388608]{0:T(1024)(128)(4,1)}), s8[4194304]{0:T(1024)(128)(4,1)S(1)}, s32[]{:S(2)}) async-start(s8[8388608]{0:T(1024)(128)(4,1)} %bitcast.164), calls=%async_computation.35 | async-start | bytes 8388608
  517.1 7.2 slice-start.1
  533.0 59.9 %reduce-scatter.22.cloned.1.call-start = ((), (), s32[]{:S(2)}) async-start(), calls=%async_computation.25 | async-start | bytes 1572864 | tf_op jit(solution)/shard_map/reduce_scatter | solution.py:249
  533.1 9.6 slice-start.2
  533.1 8.8 copy-start.8
  533.1 8.8 copy-start.10
  533.1 9.6 slice-start.3
  554.6 93.0 %reduce-scatter.40.cloned.1.call-start = ((), (), s32[]{:S(2)}) async-start(), calls=%async_computation.34 | async-start | bytes 2359296
  564.9 153.1 %reduce-scatter.38.cloned.1.call-start = ((), (), s32[]{:S(2)}) async-start(), calls=%async_computation.33 | async-start | bytes 2359296 | tf_op jit(solution)/shard_map/reduce_scatter | solution.py:305
  570.9 6.1 copy-start.28
  570.9 217.2 %reduce-scatter.36.cloned.1.call-start = ((), (), s32[]{:S(2)}) async-start(), calls=%async_computation.32 | async-start | bytes 2359296 | tf_op jit(solution)/shard_map/reduce_scatter | solution.py:302
  576.9 275.5 %reduce-scatter.34.cloned.1.call-start = ((), (), s32[]{:S(2)}) async-start(), calls=%async_computation.31 | async-start | bytes 589824 | tf_op jit(solution)/shard_map/reduce_scatter | solution.py:297
  580.2 336.8 %reduce-scatter.32.cloned.1.call-start = ((), (), s32[]{:S(2)}) async-start(), calls=%async_computation.30 | async-start | bytes 589824 | tf_op jit(solution)/shard_map/reduce_scatter | solution.py:294
  588.0 6.1 copy-start.26
  588.0 393.8 %reduce-scatter.30.cloned.1.call-start = ((), (), s32[]{:S(2)}) async-start(), calls=%async_computation.29 | async-start | bytes 589824 | tf_op jit(solution)/shard_map/reduce_scatter | solution.py:291
  594.1 4.3 copy-start.58
  600.0 447.0 %reduce-scatter.28.cloned.1.call-start = ((), (), s32[]{:S(2)}) async-start(), calls=%async_computation.28 | async-start | bytes 589824 | tf_op jit(solution)/shard_map/reduce_scatter | solution.py:288
  605.9 486.9 %reduce-scatter.26.cloned.1.call-start = ((), (), s32[]{:S(2)}) async-start(), calls=%async_computation.27 | async-start | bytes 5242880 | tf_op jit(solution)/shard_map/reduce_scatter | solution.py:39
  611.5 529.1 %reduce-scatter.18.cloned.1.call-start = ((), (), s32[]{:S(2)}) async-start(), calls=%async_computation.21 | async-start | bytes 5242880 | tf_op jit(solution)/shard_map/reduce_scatter | solution.py:39
  618.2 171.7 %copy-start.51 = (f32[4]{0:T(128)S(1)}, f32[4]{0:T(128)}, u32[]{:S(2)}) copy-start(f32[4]{0:T(128)} %get-tuple-element.202) | copy-start | bytes 52
  618.2 171.7 %copy-start.52 = (f32[4]{0:T(128)S(1)}, f32[4]{0:T(128)}, u32[]{:S(2)}) copy-start(f32[4]{0:T(128)} %get-tuple-element.203) | copy-start | bytes 52
  618.2 474.6 %copy-start.34 = (f32[1024]{0:T(1024)S(1)}, f32[1024]{0:T(1024)}, u32[]{:S(2)}) copy-start(f32[1024]{0:T(1024)} %copy-done.33) | copy-start | bytes 12292
  618.2 474.6 %copy-start.46 = (f32[2,128]{1,0:T(2,128)S(1)}, f32[2,128]{1,0:T(2,128)}, u32[]{:S(2)}) copy-start(f32[2,128]{1,0:T(2,128)} %copy-done.45) | copy-start | bytes 3076
  618.2 476.2 %copy-start.44 = (f32[1024]{0:T(1024)S(1)}, f32[1024]{0:T(1024)}, u32[]{:S(2)}) copy-start(f32[1024]{0:T(1024)} %get-tuple-element.204) | copy-start | bytes 12292
  618.2 516.6 %copy-start.48 = (f32[2,128]{1,0:T(2,128)S(1)}, f32[2,128]{1,0:T(2,128)}, u32[]{:S(2)}) copy-start(f32[2,128]{1,0:T(2,128)} %copy-done.47) | copy-start | bytes 3076
  618.2 522.4 %copy-start.5 = (f32[2,128,1024]{2,1,0:T(8,128)S(1)}, f32[2,128,1024]{2,1,0:T(8,128)}, u32[]{:S(2)}) copy-start(f32[2,128,1024]{2,1,0:T(8,128)} %reduce-scatter.20.cloned.1.call-done) | copy-start | bytes 3145732
  618.3 522.4 %copy-start.32 = (f32[1024]{0:T(1024)S(1)}, f32[1024]{0:T(1024)}, u32[]{:S(2)}) copy-start(f32[1024]{0:T(1024)} %copy-done.31) | copy-start | bytes 12292
  618.3 522.4 %copy-start.42 = (f32[2,128]{1,0:T(2,128)S(1)}, f32[2,128]{1,0:T(2,128)}, u32[]{:S(2)}) copy-start(f32[2,128]{1,0:T(2,128)} %copy-done.41) | copy-start | bytes 3076
  618.3 522.4 %copy-start.50 = (f32[2,128]{1,0:T(2,128)S(1)}, f32[2,128]{1,0:T(2,128)}, u32[]{:S(2)}) copy-start(f32[2,128]{1,0:T(2,128)} %copy-done.49) | copy-start | bytes 3076
  (25 other events, 60.5 us)
Sparse Core Ops, SparseCore 0:
  13.3 25.2 all-gather.9
  148.3 22.1 all-gather.11
  172.7 21.2 all-gather.13
  220.1 44.5 reduce-scatter.15
  438.7 42.9 reduce-scatter.19
  533.1 20.3 reduce-scatter.23
  555.8 20.3 reduce-scatter.21
  579.7 67.8 reduce-scatter.39
  651.1 66.8 reduce-scatter.37
  721.4 66.6 reduce-scatter.35
  791.5 60.9 reduce-scatter.33
  856.0 60.9 reduce-scatter.31
  920.9 60.8 reduce-scatter.29
  986.0 60.9 reduce-scatter.27
  1049.3 43.4 reduce-scatter.25
  1095.4 45.2 reduce-scatter.17
Sparse Core Ops, SparseCore 1:
  222.9 49.3 all-gather.19
  274.3 20.9 all-gather.15
  297.5 49.3 all-gather.17
  348.5 20.9 all-gather.23
  371.8 49.3 all-gather.21
  486.3 22.4 all-gather.25
where the time goes:
time: 1160 us; the launch traced here: 1150 us
  waiting for transfers between devices  750 us (65%)
  blocking collectives  168 us (14%)
  matrix products  124 us (11%)
  other arithmetic  56.5 us (5%)
  local copies, waits for them, and re-layouts  33 us (3%)
  between operations  16.9 us (1%)
    reduce_scatter x4, waiting for transfers between devices, scatter_rows(): return lax.psum_scatter(values, 'tp', scatter_dimension=1, tiled=True)  137 us
    reduce_scatter x1, waiting for transfers between devices, shards(): lax.psum_scatter(up_local.astype(jnp.bfloat16), ('fsdp', 'ctx'), scatter_...  68.4 us
    reduce_scatter x1, waiting for transfers between devices, shards(): lax.psum_scatter(gate_local.astype(jnp.bfloat16), ('fsdp', 'ctx'), scatte...  68.3 us
    reduce_scatter x1, waiting for transfers between devices, shards(): lax.psum_scatter(query_local.astype(jnp.bfloat16), ('fsdp', 'ctx'), scatt...  63.6 us
    reduce_scatter x1, waiting for transfers between devices, shards(): lax.psum_scatter(key_local.astype(jnp.bfloat16), ('fsdp', 'ctx'), scatter...  63.3 us
    reduce_scatter x1, waiting for transfers between devices, shards(): lax.psum_scatter(value_local.astype(jnp.bfloat16), ('fsdp', 'ctx'), scatt...  63 us
    reduce_scatter x1, waiting for transfers between devices, shards(): lax.psum_scatter(out_local.astype(jnp.bfloat16), ('fsdp', 'ctx'), scatter...  62.4 us
    all_gather x4, waiting for transfers between devices, gather_rows(): return lax.all_gather(values, 'tp', axis=1, tiled=True)  61.4 us
  transfers between devices with their start and end apart: 22, of which 19 were waited for; matrix products, arithmetic and copies ran while one was open for 11% of the time, Pallas kernels for 0%

commit v1 on v0

--- a/solution.py
+++ b/solution.py
@@ -7,6 +7,11 @@
 HEAD = 64
 EPS = 1e-05
 NEG = -1e30
+
+
+def one_after_other(x, inner_axis, outer_axis):
+    partial = lax.psum(x, inner_axis)
+    return lax.psum(partial, outer_axis)
 
 
 def rms_norm(values, gain):
@@ -313,8 +318,8 @@
     bias_full = lax.dynamic_update_slice_in_dim(
         jnp.zeros((2, HEADS), jnp.float32), d_bias, head_offset, 1
     )
-    attn_gain_grad, ffn_gain_grad, bias_total = lax.psum(
-        (d_gain_one, d_gain_two, bias_full), ("fsdp", "ctx", "tp")
+    attn_gain_grad, ffn_gain_grad, bias_total = one_after_other(
+        (d_gain_one, d_gain_two, bias_full), ("ctx", "tp"), "fsdp"
     )
     bias_grad = lax.dynamic_slice_in_dim(bias_total, head_offset, local_heads, 1)
     return (

time: 1160 us -> 1160 us (level)
  blocking collectives: 168 us -> 154 us
  waiting for transfers between devices: 750 us -> 763 us
    psum x1 -> x2, blocking collectives: 39.8 us -> 25.8 us  [the longest x1 13.2 us: one_after_other(): partial = lax.psum(x, inner_axis)]
    reduce_scatter x4, waiting for transfers between devices: 137 us -> 150 us  [scatter_rows(): return lax.psum_scatter(values, 'tp', scatter_dimension=1, tiled=True)]
where the time goes in v1:
time: 1160 us; the launch traced here: 1150 us
  waiting for transfers between devices  763 us (66%)
  blocking collectives  154 us (13%)
  matrix products  124 us (11%)
  other arithmetic  56.5 us (5%)
  local copies, waits for them, and re-layouts  33 us (3%)
  between operations  16.7 us (1%)
    reduce_scatter x4, waiting for transfers between devices, scatter_rows(): return lax.psum_scatter(values, 'tp', scatter_dimension=1, tiled=True)  150 us
    reduce_scatter x1, waiting for transfers between devices, shards(): lax.psum_scatter(gate_local.astype(jnp.bfloat16), ('fsdp', 'ctx'), scatte...  68.3 us
    reduce_scatter x1, waiting for transfers between devices, shards(): lax.psum_scatter(up_local.astype(jnp.bfloat16), ('fsdp', 'ctx'), scatter_...  68 us
    reduce_scatter x1, waiting for transfers between devices, shards(): lax.psum_scatter(query_local.astype(jnp.bfloat16), ('fsdp', 'ctx'), scatt...  63.6 us
    reduce_scatter x1, waiting for transfers between devices, shards(): lax.psum_scatter(key_local.astype(jnp.bfloat16), ('fsdp', 'ctx'), scatter...  63.4 us
    reduce_scatter x1, waiting for transfers between devices, shards(): lax.psum_scatter(value_local.astype(jnp.bfloat16), ('fsdp', 'ctx'), scatt...  63 us
    reduce_scatter x1, waiting for transfers between devices, shards(): lax.psum_scatter(out_local.astype(jnp.bfloat16), ('fsdp', 'ctx'), scatter...  62.4 us
    all_gather x4, waiting for transfers between devices, gather_rows(): return lax.all_gather(values, 'tp', axis=1, tiled=True)  61.2 us
  transfers between devices with their start and end apart: 22, of which 19 were waited for; matrix products, arithmetic and copies ran while one was open for 11% of the time, Pallas kernels for 0%

profile of v1, /device:TPU:0, one launch (start us, length us, event | category | flops | bytes accessed | tf_op | source)
XLA Modules:
  0.0 1149.6 jit_solution(5400061516866374129)
XLA Ops:
  15.6 33.3 %all_gather.49 = bf16[1024,256]{1,0:T(8,128)(2,1)S(1)} all-gather(bf16[128,256]{1,0:T(8,128)(2,1)} %param.18), channel_id=1, replica_groups=mesh['fsdp'=4,'ctx'=2,'tp'=4] {'fsdp','ctx'}, dimensions={0}, use_global_device_ids=true | all-gather | bytes 589824 | tf_op jit(solution)/shard_map/all_gather | solution.py:86
  49.0 31.6 %all_gather.50 = bf16[1024,256]{1,0:T(8,128)(2,1)S(1)} all-gather(bf16[128,256]{1,0:T(8,128)(2,1)} %param.19), channel_id=1, replica_groups=mesh['fsdp'=4,'ctx'=2,'tp'=4] {'fsdp','ctx'}, dimensions={0}, use_global_device_ids=true | all-gather | bytes 589824 | tf_op jit(solution)/shard_map/all_gather | solution.py:87
  80.5 31.9 %all_gather.47 = bf16[1024,256]{1,0:T(8,128)(2,1)S(1)} all-gather(bf16[128,256]{1,0:T(8,128)(2,1)} %param.20), channel_id=1, replica_groups=mesh['fsdp'=4,'ctx'=2,'tp'=4] {'fsdp','ctx'}, dimensions={0}, use_global_device_ids=true | all-gather | bytes 589824 | tf_op jit(solution)/shard_map/all_gather | solution.py:88
  112.4 31.6 %all_gather.52 = bf16[1024,256]{1,0:T(8,128)(2,1)S(1)} all-gather(bf16[128,256]{1,0:T(8,128)(2,1)} %param.21), channel_id=1, replica_groups=mesh['fsdp'=4,'ctx'=2,'tp'=4] {'fsdp','ctx'}, dimensions={0}, use_global_device_ids=true | all-gather | bytes 589824 | tf_op jit(solution)/shard_map/all_gather | solution.py:89
  145.0 3.3 convolution_convert_fusion.5
  148.8 2.5 fusion.20
  156.4 14.3 %all-gather.12.cloned.1.call-done = bf16[2,1024,256]{2,1,0:T(8,128)(2,1)} async-done(((bf16[2,512,256]{2,1,0:T(8,128)(2,1)}), bf16[2,1024,256]{2,1,0:T(8,128)(2,1)}) %all-gather.12.cloned.1.call-update) | async-done | bytes 1048592 | tf_op jit(solution)/shard_map/all_gather | solution.py:106
  170.6 2.2 fusion.65
  174.9 2.0 copy.54
  176.9 17.2 %all-gather.14.cloned.1.call-done = bf16[2,1024,256]{1,2,0:T(8,128)(2,1)} async-done(((bf16[2,512,256]{1,2,0:T(8,128)(2,1)}), bf16[2,1024,256]{1,2,0:T(8,128)(2,1)}) %all-gather.14.cloned.1.call-update) | async-done | bytes 1048592 | tf_op jit(solution)/shard_map/all_gather | solution.py:105
  194.1 2.1 fusion.64
  196.1 4.1 fusion.69
  203.6 2.8 fusion.38
  207.5 4.2 fusion.70
  215.0 2.1 fusion.39
  217.3 2.7 fusion.48
  221.0 43.8 %reduce-scatter.16.cloned.1.call-done = f32[2,128,1024]{2,1,0:T(8,128)} async-done(((f32[2,512,1024]{2,1,0:T(8,128)}), f32[2,128,1024]{2,1,0:T(8,128)}) %reduce-scatter.16.cloned.1.call-update) | async-done | bytes 1048592 | tf_op jit(solution)/shard_map/reduce_scatter | solution.py:44
  269.4 2.9 all-gather.20.cloned.1.call-done
  272.3 23.0 %all-gather.16.cloned.1.call-done = bf16[2,512,1024]{2,1,0:T(8,128)(2,1)} async-done(((bf16[2,128,1024]{2,1,0:T(8,128)(2,1)}), bf16[2,512,1024]{2,1,0:T(8,128)(2,1)}) %all-gather.16.cloned.1.call-update) | async-done | bytes 2097168 | tf_op jit(solution)/shard_map/all_gather | solution.py:40
  295.3 6.6 fusion.72
  301.9 45.0 %all-gather.18.cloned.1.call-done = bf16[1024,1024]{1,0:T(8,128)(2,1)} async-done(((bf16[128,1024]{1,0:T(8,128)(2,1)}), bf16[1024,1024]{1,0:T(8,128)(2,1)}) %all-gather.18.cloned.1.call-update) | async-done | bytes 2097168 | tf_op jit(solution)/shard_map/all_gather | solution.py:153
  346.9 6.5 fusion.71
  353.4 16.1 %all-gather.24.cloned.1.call-done = bf16[2,512,1024]{2,1,0:T(8,128)(2,1)} async-done(((bf16[2,128,1024]{2,1,0:T(8,128)(2,1)}), bf16[2,512,1024]{2,1,0:T(8,128)(2,1)}) %all-gather.24.cloned.1.call-update) | async-done | bytes 2097168 | tf_op jit(solution)/shard_map/all_gather | solution.py:40
  369.5 51.7 %all-gather.22.cloned.1.call-done = bf16[1024,1024]{1,0:T(8,128)(2,1)} async-done(((bf16[128,1024]{1,0:T(8,128)(2,1)}), bf16[1024,1024]{1,0:T(8,128)(2,1)}) %all-gather.22.cloned.1.call-update) | async-done | bytes 2097168 | tf_op jit(solution)/shard_map/all_gather | solution.py:155
  421.3 9.9 multiply_convert_fusion.2
  431.1 2.4 fusion.74
  434.2 4.4 convolution_add_fusion
  438.7 43.1 %reduce-scatter.20.cloned.1.call-done = f32[2,128,1024]{2,1,0:T(8,128)} async-done(((f32[2,512,1024]{2,1,0:T(8,128)}), f32[2,128,1024]{2,1,0:T(8,128)}) %reduce-scatter.20.cloned.1.call-update) | async-done | bytes 1048592 | tf_op jit(solution)/shard_map/reduce_scatter | solution.py:44
  481.8 2.1 multiply_reduce_fusion.2
  483.9 2.3 fusion.53
  486.8 22.0 %all-gather.26.cloned.1.call-done = bf16[2,512,1024]{2,1,0:T(8,128)(2,1)} async-done(((bf16[2,128,1024]{2,1,0:T(8,128)(2,1)}), bf16[2,512,1024]{2,1,0:T(8,128)(2,1)}) %all-gather.26.cloned.1.call-update) | async-done | bytes 2097168 | tf_op jit(solution)/shard_map/all_gather | solution.py:40
  508.8 2.4 convolution_convert_fusion.4
  511.3 5.8 fusion.24
  517.1 7.2 multiply_reduce_fusion.1
  524.4 2.3 fusion.27
  528.7 2.0 copy.59
  530.7 2.3 pad_maximum_fusion.1
  533.2 8.7 fusion
  543.3 2.6 multiply_reduce_fusion
  545.9 4.8 fusion.2
  554.9 6.0 convert_bitcast_fusion
  560.8 4.0 copy.67
  564.9 5.9 convolution_convert_fusion
  570.9 5.9 convolution_convert_fusion.1
  576.9 3.1 fusion.33
  580.1 4.5 fusion.36
  584.7 3.2 fusion.32
  588.2 4.5 fusion.37
  594.0 2.8 multiply_add_fusion.1
  602.6 3.1 convolution_convert_fusion.3
  608.6 2.7 add_add_fusion
  611.4 6.7 fusion.73
  618.2 29.1 %reduce-scatter.40.cloned.1.call-done = bf16[128,1024]{1,0:T(8,128)(2,1)} async-done(((bf16[1024,1024]{1,0:T(8,128)(2,1)}), bf16[128,1024]{1,0:T(8,128)(2,1)}) %reduce-scatter.40.cloned.1.call-update) | async-done | bytes 262160
  649.4 68.0 %reduce-scatter.38.cloned.1.call-done = bf16[128,1024]{1,0:T(8,128)(2,1)} async-done(((bf16[1024,1024]{1,0:T(8,128)(2,1)}), bf16[128,1024]{1,0:T(8,128)(2,1)}) %reduce-scatter.38.cloned.1.call-update) | async-done | bytes 262160 | tf_op jit(solution)/shard_map/reduce_scatter | solution.py:310
  719.2 68.3 %reduce-scatter.36.cloned.1.call-done = bf16[128,1024]{1,0:T(8,128)(2,1)} async-done(((bf16[1024,1024]{1,0:T(8,128)(2,1)}), bf16[128,1024]{1,0:T(8,128)(2,1)}) %reduce-scatter.36.cloned.1.call-update) | async-done | bytes 262160 | tf_op jit(solution)/shard_map/reduce_scatter | solution.py:307
  789.5 62.4 %reduce-scatter.34.cloned.1.call-done = bf16[128,256]{1,0:T(8,128)(2,1)} async-done(((bf16[1024,256]{1,0:T(8,128)(2,1)}), bf16[128,256]{1,0:T(8,128)(2,1)}) %reduce-scatter.34.cloned.1.call-update) | async-done | bytes 65552 | tf_op jit(solution)/shard_map/reduce_scatter | solution.py:302
  853.3 63.0 %reduce-scatter.32.cloned.1.call-done = bf16[128,256]{1,0:T(8,128)(2,1)} async-done(((bf16[1024,256]{1,0:T(8,128)(2,1)}), bf16[128,256]{1,0:T(8,128)(2,1)}) %reduce-scatter.32.cloned.1.call-update) | async-done | bytes 65552 | tf_op jit(solution)/shard_map/reduce_scatter | solution.py:299
  917.8 63.4 %reduce-scatter.30.cloned.1.call-done = bf16[128,256]{1,0:T(8,128)(2,1)} async-done(((bf16[1024,256]{1,0:T(8,128)(2,1)}), bf16[128,256]{1,0:T(8,128)(2,1)}) %reduce-scatter.30.cloned.1.call-update) | async-done | bytes 65552 | tf_op jit(solution)/shard_map/reduce_scatter | solution.py:296
  982.7 63.6 %reduce-scatter.28.cloned.1.call-done = bf16[128,256]{1,0:T(8,128)(2,1)} async-done(((bf16[1024,256]{1,0:T(8,128)(2,1)}), bf16[128,256]{1,0:T(8,128)(2,1)}) %reduce-scatter.28.cloned.1.call-update) | async-done | bytes 65552 | tf_op jit(solution)/shard_map/reduce_scatter | solution.py:293
  1047.8 44.4 %reduce-scatter.26.cloned.1.call-done = f32[2,128,1024]{2,1,0:T(8,128)} async-done(((f32[2,512,1024]{2,1,0:T(8,128)}), f32[2,128,1024]{2,1,0:T(8,128)}) %reduce-scatter.26.cloned.1.call-update) | async-done | bytes 1048592 | tf_op jit(solution)/shard_map/reduce_scatter | solution.py:44
  1093.7 13.2 %all-reduce.4 = (f32[1024]{0:T(1024)S(1)}, f32[1024]{0:T(1024)S(1)}, f32[2,16]{1,0:T(2,128)S(1)}) all-reduce(f32[1024]{0:T(1024)S(1)} %get-tuple-element.206, f32[1024]{0:T(1024)S(1)} %copy-done.44, f32[2,16]{1,0:T(2,128)S(1)} %dynamic_update_slice.18), channel_id=1, replica_groups=mesh['fsdp'=4,'ctx'=2,'tp'=4] {'ctx','tp'}, use_global_device_ids=true, to_apply=%region_17.18 | all-reduce | flops 2080 | bytes 16640 | tf_op jit(solution)/shard_map/psum | solution.py:13
  1106.9 12.6 %all-reduce.5 = (f32[1024]{0:T(1024)}, f32[1024]{0:T(1024)}, f32[2,16]{1,0:T(2,128)S(1)}) all-reduce(f32[1024]{0:T(1024)S(1)} %get-tuple-element.224, f32[1024]{0:T(1024)S(1)} %get-tuple-element.225, f32[2,16]{1,0:T(2,128)S(1)} %get-tuple-element.226), channel_id=1, replica_groups=mesh['fsdp'=4,'ctx'=2,'tp'=4] {'fsdp'}, use_global_device_ids=true, to_apply=%region_18.19 | all-reduce | flops 2080 | bytes 16640 | tf_op jit(solution)/shard_map/psum | solution.py:14
  1120.2 19.1 %reduce-scatter.18.cloned.1.call-done = f32[2,128,1024]{2,1,0:T(8,128)} async-done(((f32[2,512,1024]{2,1,0:T(8,128)}), f32[2,128,1024]{2,1,0:T(8,128)}) %reduce-scatter.18.cloned.1.call-update) | async-done | bytes 1048592 | tf_op jit(solution)/shard_map/reduce_scatter | solution.py:44
  1139.3 3.0 fusion.44
  (244 shorter events, 62.6 us)
Async XLA Ops:
  8.0 136.9 %all-gather.10.cloned.1.call-start = ((), (), s32[]{:S(2)}) async-start(), calls=%async_computation.13 | async-start | bytes 2621440 | tf_op jit(solution)/shard_map/all_gather | solution.py:40
  13.2 157.4 %all-gather.12.cloned.1.call-start = ((), (), s32[]{:S(2)}) async-start(), calls=%async_computation.14 | async-start | bytes 1572864 | tf_op jit(solution)/shard_map/all_gather | solution.py:106
  80.5 67.8 %copy-start.43 = (s32[2,1024]{1,0:T(2,128)S(1)}, s32[2,1024]{1,0:T(2,128)}, u32[]{:S(2)}) copy-start(s32[2,1024]{1,0:T(2,128)} %param.26) | copy-start | bytes 24580
  112.4 36.2 %copy-start.23 = (bf16[1024,256]{1,0:T(8,128)(2,1)}, bf16[1024,256]{1,0:T(8,128)(2,1)S(1)}, u32[]{:S(2)}) copy-start(bf16[1024,256]{1,0:T(8,128)(2,1)S(1)} %all_gather.47) | copy-start | bytes 1572868
  144.0 73.3 %copy-start.13 = (bf16[1024,256]{1,0:T(8,128)(2,1)}, bf16[1024,256]{1,0:T(8,128)(2,1)S(1)}, u32[]{:S(2)}) copy-start(bf16[1024,256]{1,0:T(8,128)(2,1)S(1)} %all_gather.52) | copy-start | bytes 1572868
  144.5 7.5 copy-start.25
  144.9 51.2 %copy-start.11 = (pred[512,1024]{1,0:T(8,128)(4,1)}, pred[512,1024]{1,0:T(8,128)(4,1)S(1)}, u32[]{:S(2)}) copy-start(pred[512,1024]{1,0:T(8,128)(4,1)S(1)} %broadcast_compare_fusion) | copy-start | bytes 1572868
  148.3 45.8 %all-gather.14.cloned.1.call-start = ((), (), s32[]{:S(2)}) async-start(), calls=%async_computation.15 | async-start | bytes 1572864 | tf_op jit(solution)/shard_map/all_gather | solution.py:105
  152.4 55.0 %copy-start.7 = (bf16[2,512,4,32]{1,3,2,0:T(8,128)(2,1)}, bf16[2,512,4,32]{1,3,2,0:T(8,128)(2,1)S(1)}, u32[]{:S(2)}) copy-start(bf16[2,512,4,32]{1,3,2,0:T(8,128)(2,1)S(1)} %get-tuple-element.241) | copy-start | bytes 786436
  152.4 55.0 %copy-start.9 = (bf16[2,512,4,32]{1,3,2,0:T(8,128)(2,1)}, bf16[2,512,4,32]{1,3,2,0:T(8,128)(2,1)S(1)}, u32[]{:S(2)}) copy-start(bf16[2,512,4,32]{1,3,2,0:T(8,128)(2,1)S(1)} %get-tuple-element.242) | copy-start | bytes 786436
  153.4 111.4 %reduce-scatter.16.cloned.1.call-start = ((), (), s32[]{:S(2)}) async-start(), calls=%async_computation.16 | async-start | bytes 5242880 | tf_op jit(solution)/shard_map/reduce_scatter | solution.py:44
  153.7 46.6 %copy-start.55 = (f32[4]{0:T(128)}, f32[4]{0:T(128)S(1)}, u32[]{:S(2)}) copy-start(f32[4]{0:T(128)S(1)} %get-tuple-element.267) | copy-start | bytes 52
  153.7 46.6 %copy-start.56 = (f32[4]{0:T(128)}, f32[4]{0:T(128)S(1)}, u32[]{:S(2)}) copy-start(f32[4]{0:T(128)S(1)} %get-tuple-element.268) | copy-start | bytes 52
  154.0 53.4 %copy-start.14 = (pred[512,1024]{1,0:T(8,128)(4,1)}, pred[512,1024]{1,0:T(8,128)(4,1)S(1)}, u32[]{:S(2)}) copy-start(pred[512,1024]{1,0:T(8,128)(4,1)S(1)} %broadcast_compare_fusion.2) | copy-start | bytes 1572868
  196.1 4.1 copy-start.22
  202.1 4.2 copy-start.35
  207.4 9.9 copy-start.27
  217.3 47.5 %copy-start.4 = (bf16[2,128,1024]{2,1,0:T(8,128)(2,1)S(1)}, bf16[2,128,1024]{2,1,0:T(8,128)(2,1)}, u32[]{:S(2)}) copy-start(bf16[2,128,1024]{2,1,0:T(8,128)(2,1)} %param.15) | copy-start | bytes 1572868
  220.1 52.2 %all-gather.20.cloned.1.call-start = ((), (), s32[]{:S(2)}) async-start(), calls=%async_computation.19 | async-start | bytes 2359296 | tf_op jit(solution)/shard_map/all_gather | solution.py:154
  220.7 74.7 %all-gather.16.cloned.1.call-start = ((), (), s32[]{:S(2)}) async-start(), calls=%async_computation.17 | async-start | bytes 2621440 | tf_op jit(solution)/shard_map/all_gather | solution.py:40
  221.0 262.9 %copy-start.31 = (f32[1024]{0:T(1024)}, f32[1024]{0:T(1024)S(1)}, u32[]{:S(2)}) copy-start(f32[1024]{0:T(1024)S(1)} %convert_element_type.167) | copy-start | bytes 12292
  266.3 217.6 %copy-start.41 = (f32[2,128]{1,0:T(2,128)}, f32[2,128]{1,0:T(2,128)S(1)}, u32[]{:S(2)}) copy-start(f32[2,128]{1,0:T(2,128)S(1)} %fusion.57) | copy-start | bytes 3076
  267.2 79.7 %all-gather.18.cloned.1.call-start = ((), (), s32[]{:S(2)}) async-start(), calls=%async_computation.18 | async-start | bytes 2359296 | tf_op jit(solution)/shard_map/all_gather | solution.py:153
  267.8 101.7 %all-gather.24.cloned.1.call-start = ((), (), s32[]{:S(2)}) async-start(), calls=%async_computation.22 | async-start | bytes 2621440 | tf_op jit(solution)/shard_map/all_gather | solution.py:40
  268.6 152.7 %all-gather.22.cloned.1.call-start = ((), (), s32[]{:S(2)}) async-start(), calls=%async_computation.20 | async-start | bytes 2359296 | tf_op jit(solution)/shard_map/all_gather | solution.py:155
  269.3 212.5 %reduce-scatter.20.cloned.1.call-start = ((), (), s32[]{:S(2)}) async-start(), calls=%async_computation.23 | async-start | bytes 5242880 | tf_op jit(solution)/shard_map/reduce_scatter | solution.py:44
  421.3 9.9 copy-start.60
  438.6 45.2 %copy-start.6 = (bf16[2,128,1024]{2,1,0:T(8,128)(2,1)S(1)}, bf16[2,128,1024]{2,1,0:T(8,128)(2,1)}, u32[]{:S(2)}) copy-start(bf16[2,128,1024]{2,1,0:T(8,128)(2,1)} %param.29) | copy-start | bytes 1572868
  438.6 48.1 %copy-start.36 = (f32[4,512]{1,0:T(4,128)S(1)}, f32[4,512]{1,0:T(4,128)}, u32[]{:S(2)}) copy-start(f32[4,512]{1,0:T(4,128)} %copy-done.35) | copy-start | bytes 24580
  438.6 48.1 %copy-start.38 = (f32[4,512]{1,0:T(4,128)S(1)}, f32[4,512]{1,0:T(4,128)}, u32[]{:S(2)}) copy-start(f32[4,512]{1,0:T(4,128)} %copy-done.37) | copy-start | bytes 24580
  438.6 48.1 %copy-start.40 = (f32[4,512]{1,0:T(4,128)S(1)}, f32[4,512]{1,0:T(4,128)}, u32[]{:S(2)}) copy-start(f32[4,512]{1,0:T(4,128)} %copy-done.39) | copy-start | bytes 24580
  438.6 70.1 %all-gather.26.cloned.1.call-start = ((), (), s32[]{:S(2)}) async-start(), calls=%async_computation.24 | async-start | bytes 2621440 | tf_op jit(solution)/shard_map/all_gather | solution.py:40
  483.9 24.9 %copy-start.49 = (f32[2,128]{1,0:T(2,128)}, f32[2,128]{1,0:T(2,128)S(1)}, u32[]{:S(2)}) copy-start(f32[2,128]{1,0:T(2,128)S(1)} %multiply_multiply_fusion.1) | copy-start | bytes 3076
  486.2 98.5 %reduce-scatter.24.cloned.1.call-start = ((), (), s32[]{:S(2)}) async-start(), calls=%async_computation.26 | async-start | bytes 1572864 | tf_op jit(solution)/shard_map/reduce_scatter | solution.py:257
  511.3 5.9 copy-start.18
  511.3 13.1 %slice-start = ((s8[8388608]{0:T(1024)(128)(4,1)}), s8[4194304]{0:T(1024)(128)(4,1)S(1)}, s32[]{:S(2)}) async-start(s8[8388608]{0:T(1024)(128)(4,1)} %bitcast.164), calls=%async_computation.35 | async-start | bytes 8388608
  517.1 7.3 slice-start.1
  533.1 59.7 %reduce-scatter.22.cloned.1.call-start = ((), (), s32[]{:S(2)}) async-start(), calls=%async_computation.25 | async-start | bytes 1572864 | tf_op jit(solution)/shard_map/reduce_scatter | solution.py:254
  533.1 9.6 slice-start.2
  533.1 8.8 copy-start.8
  533.1 8.8 copy-start.10
  533.1 9.6 slice-start.3
  554.6 92.7 %reduce-scatter.40.cloned.1.call-start = ((), (), s32[]{:S(2)}) async-start(), calls=%async_computation.34 | async-start | bytes 2359296
  564.9 152.5 %reduce-scatter.38.cloned.1.call-start = ((), (), s32[]{:S(2)}) async-start(), calls=%async_computation.33 | async-start | bytes 2359296 | tf_op jit(solution)/shard_map/reduce_scatter | solution.py:310
  570.9 6.1 copy-start.28
  570.9 216.6 %reduce-scatter.36.cloned.1.call-start = ((), (), s32[]{:S(2)}) async-start(), calls=%async_computation.32 | async-start | bytes 2359296 | tf_op jit(solution)/shard_map/reduce_scatter | solution.py:307
  576.9 275.0 %reduce-scatter.34.cloned.1.call-start = ((), (), s32[]{:S(2)}) async-start(), calls=%async_computation.31 | async-start | bytes 589824 | tf_op jit(solution)/shard_map/reduce_scatter | solution.py:302
  580.1 336.3 %reduce-scatter.32.cloned.1.call-start = ((), (), s32[]{:S(2)}) async-start(), calls=%async_computation.30 | async-start | bytes 589824 | tf_op jit(solution)/shard_map/reduce_scatter | solution.py:299
  587.9 6.0 copy-start.26
  588.0 393.3 %reduce-scatter.30.cloned.1.call-start = ((), (), s32[]{:S(2)}) async-start(), calls=%async_computation.29 | async-start | bytes 589824 | tf_op jit(solution)/shard_map/reduce_scatter | solution.py:296
  593.9 4.3 copy-start.58
  599.9 446.4 %reduce-scatter.28.cloned.1.call-start = ((), (), s32[]{:S(2)}) async-start(), calls=%async_computation.28 | async-start | bytes 589824 | tf_op jit(solution)/shard_map/reduce_scatter | solution.py:293
  605.8 486.4 %reduce-scatter.26.cloned.1.call-start = ((), (), s32[]{:S(2)}) async-start(), calls=%async_computation.27 | async-start | bytes 5242880 | tf_op jit(solution)/shard_map/reduce_scatter | solution.py:44
  611.4 527.9 %reduce-scatter.18.cloned.1.call-start = ((), (), s32[]{:S(2)}) async-start(), calls=%async_computation.21 | async-start | bytes 5242880 | tf_op jit(solution)/shard_map/reduce_scatter | solution.py:44
  618.1 171.2 %copy-start.51 = (f32[4]{0:T(128)S(1)}, f32[4]{0:T(128)}, u32[]{:S(2)}) copy-start(f32[4]{0:T(128)} %get-tuple-element.202) | copy-start | bytes 52
  618.1 171.2 %copy-start.52 = (f32[4]{0:T(128)S(1)}, f32[4]{0:T(128)}, u32[]{:S(2)}) copy-start(f32[4]{0:T(128)} %get-tuple-element.203) | copy-start | bytes 52
  618.1 474.1 %copy-start.34 = (f32[1024]{0:T(1024)S(1)}, f32[1024]{0:T(1024)}, u32[]{:S(2)}) copy-start(f32[1024]{0:T(1024)} %copy-done.33) | copy-start | bytes 12292
  618.1 474.1 %copy-start.46 = (f32[2,128]{1,0:T(2,128)S(1)}, f32[2,128]{1,0:T(2,128)}, u32[]{:S(2)}) copy-start(f32[2,128]{1,0:T(2,128)} %copy-done.45) | copy-start | bytes 3076
  618.1 475.6 %copy-start.44 = (f32[1024]{0:T(1024)S(1)}, f32[1024]{0:T(1024)}, u32[]{:S(2)}) copy-start(f32[1024]{0:T(1024)} %get-tuple-element.204) | copy-start | bytes 12292
  618.1 502.1 %copy-start.48 = (f32[2,128]{1,0:T(2,128)S(1)}, f32[2,128]{1,0:T(2,128)}, u32[]{:S(2)}) copy-start(f32[2,128]{1,0:T(2,128)} %copy-done.47) | copy-start | bytes 3076
  618.1 521.1 %copy-start.5 = (f32[2,128,1024]{2,1,0:T(8,128)S(1)}, f32[2,128,1024]{2,1,0:T(8,128)}, u32[]{:S(2)}) copy-start(f32[2,128,1024]{2,1,0:T(8,128)} %reduce-scatter.20.cloned.1.call-done) | copy-start | bytes 3145732
  618.1 521.1 %copy-start.32 = (f32[1024]{0:T(1024)S(1)}, f32[1024]{0:T(1024)}, u32[]{:S(2)}) copy-start(f32[1024]{0:T(1024)} %copy-done.31) | copy-start | bytes 12292
  618.1 521.1 %copy-start.42 = (f32[2,128]{1,0:T(2,128)S(1)}, f32[2,128]{1,0:T(2,128)}, u32[]{:S(2)}) copy-start(f32[2,128]{1,0:T(2,128)} %copy-done.41) | copy-start | bytes 3076
  618.2 521.1 %copy-start.50 = (f32[2,128]{1,0:T(2,128)S(1)}, f32[2,128]{1,0:T(2,128)}, u32[]{:S(2)}) copy-start(f32[2,128]{1,0:T(2,128)} %copy-done.49) | copy-start | bytes 3076
  (25 other events, 60.3 us)
Sparse Core Ops, SparseCore 0:
  13.3 25.2 all-gather.9
  148.4 22.1 all-gather.11
  172.7 21.2 all-gather.13
  220.2 44.5 reduce-scatter.15
  438.8 42.9 reduce-scatter.19
  533.2 20.3 reduce-scatter.23
  555.9 20.2 reduce-scatter.21
  579.7 67.5 reduce-scatter.39
  650.8 66.5 reduce-scatter.37
  720.8 66.6 reduce-scatter.35
  790.8 60.9 reduce-scatter.33
  855.4 60.9 reduce-scatter.31
  920.3 60.9 reduce-scatter.29
  985.3 60.8 reduce-scatter.27
  1048.6 43.4 reduce-scatter.25
  1094.7 44.4 reduce-scatter.17
Sparse Core Ops, SparseCore 1:
  222.9 49.3 all-gather.19
  274.4 20.9 all-gather.15
  297.5 49.3 all-gather.17
  348.6 20.9 all-gather.23
  371.9 49.3 all-gather.21
  486.3 22.4 all-gather.25
